TPU v7x, 32 devices: a whole 2x2x4 slice. The times are simulated.
32 devices in a mesh: gauss: 16 (over z, x, core), tile: 2 (over y).
Axes of the slice: x: 2, y: 2, z: 4, core: 2. Of those that a mesh axis runs over, the one named last changes fastest.
Arguments:
- splats: float32 [9, 32768], P(None, ('gauss', 'tile')), may hold values from -8 to 260, as said below
- sh_coeffs: float32 [48, 32768], P(None, ('gauss', 'tile')), may hold values from -2 to 2
- send_list: int32 [32768], P(('gauss', 'tile')), may hold values from 0 to 1023, as said below
- block_slots: int32 [16, 96, 128], P('gauss', 'tile'), may hold values from 0 to 1023, as said below
- block_tiles: int32 [16, 96], P('gauss', 'tile'), may hold values from 0 to 8, as said below
- target: float32 [3, 256, 256], P(None, 'gauss', 'tile'), may hold values from 0 to 1
Outputs:
- rendered: float32 [3, 256, 256], P(None, 'gauss', 'tile')
- grad_splats: float32 [9, 32768], P(None, ('gauss', 'tile'))
- grad_sh: float32 [48, 32768], P(None, ('gauss', 'tile'))
Inputs may be any that keep to these rules, and one draw needn't show every extreme that they name: `send_list`: each device's 1024 entries are a permutation of 0 to 1023. `block_tiles`: each device's 48 entries never fall; each of its tiles 0 to 7 has at least one block; the value 8 marks an unused slot; in every draw some device uses all 48 slots. `block_slots`: entries index the device's received Gaussians. `splats`: conics are positive definite; view directions have unit length; opacity logits (row 5) lie between -8 and -2.
All inputs are finite; a program needn't handle non-finite values.
Results may differ from a plain program's by a relative error of at most 0.0003.
Values sent between devices are 32-bit elements; how exact they have to be, the bound alone decides.
A program may use at most 64 MiB of HBM per device.

v0:
```python
import jax
import jax.numpy as jnp
from jax import lax
from jax.sharding import PartitionSpec as P

TILE_SIDE = 16
TILES_DEV = 8
HIGHEST = lax.Precision.HIGHEST
BASE_ZERO = 0.28209479177387814
BASE_ONE = 0.4886025119029199
BASE_TWO = (
    1.0925484305920792,
    -1.0925484305920792,
    0.31539156525252005,
    -1.0925484305920792,
    0.5462742152960396,
)
BASE_THREE = (
    -0.5900435899266435,
    2.890611442640554,
    -0.4570457994644658,
    0.3731763325901154,
    -0.4570457994644658,
    1.445305721320277,
    -0.5900435899266435,
)
CONST_ONE = 0.0001
CONST_TWO = 0.0009


def extended(cells, sides, width):
    for axis, dim in sides:
        count = lax.axis_size(axis)
        ends = count - 1
        head = lax.slice_in_dim(cells, 0, width, axis=dim)
        tail = lax.slice_in_dim(cells, cells.shape[dim] - width, cells.shape[dim], axis=dim)
        cells = jnp.concatenate(
            [
                lax.ppermute(tail, axis, [(i, (i + 1) % count) for i in range(ends)]),
                cells,
                lax.ppermute(head, axis, [((i + 1) % count, i) for i in range(ends)]),
            ],
            axis=dim,
        )
    return cells


def harmonics(direction):
    coord_x, coord_y, coord_z = (direction[0], direction[1], direction[2])
    square_x, square_y, square_z = (coord_x * coord_x, coord_y * coord_y, coord_z * coord_z)
    rows_list = [
        jnp.full_like(coord_x, BASE_ZERO),
        -BASE_ONE * coord_y,
        BASE_ONE * coord_z,
        -BASE_ONE * coord_x,
        BASE_TWO[0] * coord_x * coord_y,
        BASE_TWO[1] * coord_y * coord_z,
        BASE_TWO[2] * (2.0 * square_z - square_x - square_y),
        BASE_TWO[3] * coord_x * coord_z,
        BASE_TWO[4] * (square_x - square_y),
        BASE_THREE[0] * coord_y * (3.0 * square_x - square_y),
        BASE_THREE[1] * coord_x * coord_y * coord_z,
        BASE_THREE[2] * coord_y * (4.0 * square_z - square_x - square_y),
        BASE_THREE[3] * coord_z * (2.0 * square_z - 3.0 * square_x - 3.0 * square_y),
        BASE_THREE[4] * coord_x * (4.0 * square_z - square_x - square_y),
        BASE_THREE[5] * coord_z * (square_x - square_y),
        BASE_THREE[6] * coord_x * (square_x - 3.0 * square_y),
    ]
    return jnp.stack(rows_list)


def shade(direction, coeffs):
    basis = harmonics(direction)
    return 0.5 + jnp.sum(coeffs.reshape(3, 16, -1) * basis[None], axis=1)


def composite(records):
    members = records.shape[1]
    pixels = jnp.arange(TILE_SIDE * TILE_SIDE)
    pixel_u = (pixels % TILE_SIDE).astype(jnp.float32)
    pixel_v = (pixels // TILE_SIDE).astype(jnp.float32)
    delta_x = pixel_u[None, :] - records[0][:, None]
    delta_y = pixel_v[None, :] - records[1][:, None]
    exponent = (
        -0.5 * (records[2][:, None] * delta_x * delta_x + records[4][:, None] * delta_y * delta_y)
        - records[3][:, None] * delta_x * delta_y
    )
    alphas = jax.nn.sigmoid(records[5])[:, None] * jnp.exp(exponent)
    logged = jnp.log1p(-alphas)
    positions = jnp.arange(members)
    earlier_mask = (positions[None, :] < positions[:, None]).astype(jnp.float32)
    before = jnp.dot(earlier_mask, logged, precision=HIGHEST, preferred_element_type=jnp.float32)
    weight = alphas * jnp.exp(before)
    colour = jnp.dot(records[6:9], weight, precision=HIGHEST, preferred_element_type=jnp.float32)
    return jnp.concatenate([colour, jnp.sum(logged, axis=0, keepdims=True)], axis=0)


def block_pullback(paired):
    unused, pulling = jax.vjp(composite, paired[0])
    return pulling(paired[1])[0]


def combine(results, tile_ids):
    positions = jnp.arange(results.shape[0])
    earlier = (
        (tile_ids[:, None] == tile_ids[None, :]) & (positions[None, :] < positions[:, None])
    ).astype(jnp.float32)
    prefix = jnp.dot(earlier, results[:, 3], precision=HIGHEST, preferred_element_type=jnp.float32)
    member = (jnp.arange(TILES_DEV)[:, None] == tile_ids[None, :]).astype(jnp.float32)
    shaded = jnp.exp(prefix)[:, None, :] * results[:, 0:3]
    return jnp.einsum("kb,bcp->kcp", member, shaded, precision=HIGHEST)


def to_image(tiles_img):
    return (
        tiles_img.reshape(TILES_DEV, 3, TILE_SIDE, TILE_SIDE)
        .transpose(1, 2, 0, 3)
        .reshape(3, TILE_SIDE, TILES_DEV * TILE_SIDE)
    )


def window():
    tap_offsets = jnp.arange(11).astype(jnp.float32) - 5.0
    profile = jnp.exp(-tap_offsets * tap_offsets / 4.5)
    return profile / jnp.sum(profile)


def blur(padded, rows_out, cols_out):
    weights = window()
    across = weights[0] * padded[..., :, 0:cols_out]
    for offset in range(1, 11):
        across = across + weights[offset] * padded[..., :, offset : offset + cols_out]
    result = weights[0] * across[..., 0:rows_out, :]
    for offset in range(1, 11):
        result = result + weights[offset] * across[..., offset : offset + rows_out, :]
    return result


def similarity(mu_x, mu_y, sq_x, sq_y, cross_xy):
    mean_xy = mu_x * mu_y
    numerator = (2.0 * mean_xy + CONST_ONE) * (2.0 * (cross_xy - mean_xy) + CONST_TWO)
    denominator = (mu_x * mu_x + mu_y * mu_y + CONST_ONE) * (
        sq_x - mu_x * mu_x + sq_y - mu_y * mu_y + CONST_TWO
    )
    return numerator / denominator


def five_products(padded):
    return jnp.stack(
        [padded[0], padded[1], padded[0] * padded[0], padded[1] * padded[1], padded[0] * padded[1]]
    )


def similarity_grads(moments):

    def partial_loss(mean_x, square_x, product_xy):
        return jnp.sum(
            0.2 * (1.0 - similarity(mean_x, moments[1], square_x, moments[3], product_xy))
        )

    return jnp.stack(jax.grad(partial_loss, argnums=(0, 1, 2))(moments[0], moments[2], moments[4]))


def run_live(apply, arrays_in, live, out_shape):

    def advance(position, buffer):
        picked = tuple(
            (lax.dynamic_index_in_dim(member, position, 0, keepdims=False) for member in arrays_in)
        )
        return lax.dynamic_update_index_in_dim(buffer, apply(picked), position, 0)

    return lax.fori_loop(0, live, advance, jnp.zeros(out_shape, jnp.float32))


def body(splats, sh_coeffs, send_list, block_slots, block_tiles, target):
    row_band = lax.axis_index("gauss")
    col_band = lax.axis_index("tile")
    owners = lax.axis_size("gauss")
    peers = lax.axis_size("tile")
    own_records = jnp.concatenate([splats[0:6], shade(splats[6:9], sh_coeffs)], axis=0)
    received = lax.all_to_all(
        own_records[:, send_list], "gauss", split_axis=1, concat_axis=1, tiled=True
    )
    tile_ids = block_tiles[0]
    slot_rows = block_slots[0]
    slots_total = slot_rows.shape[0]
    gathered = received[:, slot_rows.reshape(-1)].reshape(9, slots_total, slot_rows.shape[1])
    anchor_x = (TILE_SIDE * (TILES_DEV * col_band + jnp.minimum(tile_ids, TILES_DEV - 1))).astype(
        jnp.float32
    )
    anchor_y = (TILE_SIDE * row_band).astype(jnp.float32)
    shifted = jnp.concatenate(
        [gathered[0:1] - anchor_x[None, :, None], gathered[1:2] - anchor_y, gathered[2:9]], axis=0
    )
    per_block = jnp.moveaxis(shifted, 1, 0)
    live = jnp.sum((tile_ids < TILES_DEV).astype(jnp.int32))
    pixel_count = TILE_SIDE * TILE_SIDE
    results = run_live(
        lambda picked: composite(picked[0]), (per_block,), live, (slots_total, 4, pixel_count)
    )
    tiles_img = combine(results, tile_ids)
    rendered = to_image(tiles_img)
    rows_here = rendered.shape[1]
    cols_here = rendered.shape[2]
    padded = extended(jnp.stack([rendered, target]), (("gauss", 2), ("tile", 3)), 10)
    moments = blur(five_products(padded), rows_here + 10, cols_here + 10)
    grads_map = similarity_grads(moments)
    row_ids = row_band * rows_here - 5 + jnp.arange(rows_here + 10)
    col_ids = col_band * cols_here - 5 + jnp.arange(cols_here + 10)
    inside = ((row_ids >= 0) & (row_ids < rows_here * owners))[:, None] & (
        (col_ids >= 0) & (col_ids < cols_here * peers)
    )[None, :]
    spread = blur(grads_map * inside.astype(jnp.float32), rows_here, cols_here)
    pixel_grad = (
        spread[0] + 2.0 * rendered * spread[1] + target * spread[2] + 1.6 * (rendered - target)
    )
    tile_grad = (
        pixel_grad.reshape(3, TILE_SIDE, TILES_DEV, TILE_SIDE)
        .transpose(2, 0, 1, 3)
        .reshape(TILES_DEV, 3, pixel_count)
    )
    unused, combine_pull = jax.vjp(lambda found: combine(found, tile_ids), results)
    results_grad = combine_pull(tile_grad)[0]
    block_grad = run_live(block_pullback, (per_block, results_grad), live, per_block.shape)
    flat_grad = jnp.moveaxis(block_grad, 0, 1).reshape(9, -1)
    table_grad = jnp.zeros_like(received).at[:, slot_rows.reshape(-1)].add(flat_grad)
    back_records = lax.all_to_all(table_grad, "gauss", split_axis=1, concat_axis=1, tiled=True)
    own_grad = jnp.zeros_like(own_records).at[:, send_list].set(back_records)
    unused_colour, shade_pull = jax.vjp(shade, splats[6:9], sh_coeffs)
    dir_grad, grad_sh = shade_pull(own_grad[6:9])
    grad_splats = jnp.concatenate([own_grad[0:6], dir_grad], axis=0)
    return (rendered, grad_splats, grad_sh)


def solution(mesh):
    in_specs = (
        P(None, ("gauss", "tile")),
        P(None, ("gauss", "tile")),
        P(("gauss", "tile")),
        P("gauss", "tile", None),
        P("gauss", "tile"),
        P(None, "gauss", "tile"),
    )
    out_specs = (P(None, "gauss", "tile"), P(None, ("gauss", "tile")), P(None, ("gauss", "tile")))
    return jax.shard_map(body, mesh=mesh, in_specs=in_specs, out_specs=out_specs, check_vma=False)
```

profile of v0, /device:TPU:0, one launch (start us, length us, event | category | flops | bytes accessed | tf_op | source)
XLA Modules:
  0.0 363.7 jit_solution(15220192069105559157)
XLA Ops:
  0.6 0.9 multiply_multiply_fusion.2
  1.5 0.8 slice.409
  2.3 0.9 multiply_multiply_fusion.3
  3.3 1.0 multiply_reduce_fusion.2
  5.3 2.8 gather_fusion
  9.0 7.4 %all-to-all-start = ((f32[16,1,576]{2,1,0:T(1,128)}), f32[16,1,576]{2,1,0:T(1,128)S(1)}, u32[]{:S(2)}, u32[]{:S(2)}) async-start(f32[16,1,576]{2,1,0:T(1,128)} %reshape.453), calls=%async_computation | async-start | bytes 81920 | tf_op jit(solution)/shard_map/all_to_all | solution.py:181
  16.4 0.8 compare_select_fusion
  17.3 1.4 multiply_convert_fusion
  19.3 3.8 %all-to-all-done = f32[16,1,576]{2,1,0:T(1,128)S(1)} async-done(((f32[16,1,576]{2,1,0:T(1,128)}), f32[16,1,576]{2,1,0:T(1,128)S(1)}, u32[]{:S(2)}, u32[]{:S(2)}) %all-to-all-start) | async-done | bytes 36896 | tf_op jit(solution)/shard_map/all_to_all | solution.py:181
  24.5 1.0 copy.59
  25.5 17.1 %gather_fusion.1 = f32[6144,9]{1,0:T(8,128)S(1)} fusion(f32[9,1024]{0,1:T(8,128)} %bitcast.194, s32[6144]{0:T(1024)S(1)} %broadcast_clamp_fusion), kind=kCustom, calls=%fused_computation.1 | custom fusion | bytes 466944 | tf_op jit(solution)/shard_map/gather | solution.py:187
  42.6 2.5 slice.497
  45.2 2.5 slice_reduce_fusion
  47.7 2.4 copy.62
  50.3 24.7 %while.24 = (s32[]{:T(128)}, f32[48,4,256]{2,1,0:T(4,128)S(1)}, s32[]{:T(128)}, f32[48,9,128]{2,1,0:T(8,128)S(1)}, s32[]{:T(128)}, /*index=5*/s32[]{:T(128)}, s3...) while((s32[]{:T(128)}, f32[48,4,256]{2,1,0:T(4,128)S(1)}, s32[]{:T(128)}, f32[48,9,128]{2,1,0:T(8,128)S(1)}, ...), condition=%wide.region_4.5_spmd, body=%wide.region_2.4_spmd.sunk | while | flops 52843144 | bytes 296203 | solution.py:172
  75.9 54.4 %collective-permute-start = (f32[2,3,10,128]{3,2,1,0:T(8,128)S(1)}, f32[2,3,10,128]{3,2,1,0:T(8,128)S(1)}, u32[]{:S(2)}, u32[]{:S(2)}) collective-permute-start(f32[2,3,10,128]{3,2,1,0:T(8,128)S(1)} %get-tuple-element.234), channel_id=1, source_target_pairs={{0,2},{2,4},{4,6},{6,8},{8,10},{10,12},{12,14},{14,16},{16,18},{18... | collective-permute-start | bytes 92168 | tf_op jit(solution)/shard_map/ppermute | solution.py:39
  130.2 1.3 collective-permute-start.1
  132.1 1.5 collective-permute-done.1
  133.7 2.9 collective-permute-start.2
  136.7 1.3 collective-permute-start.3
  138.8 1.1 collective-permute-done.2
  139.9 4.7 %collective-permute-done.3 = f32[2,3,36,10]{3,2,1,0:T(8,128)S(1)} collective-permute-done((f32[2,3,36,10]{3,2,1,0:T(8,128)S(1)}, f32[2,3,36,10]{3,2,1,0:T(8,128)S(1)}, u32[]{:S(2)}, u32[]{:S(2)}) %collective-permute-start.3) | collective-permute-done | bytes 8672 | tf_op jit(solution)/shard_map/ppermute | solution.py:41
  145.0 8.4 %fusion.74 = f32[5,3,36,138]{3,2,1,0:T(8,128)S(1)} fusion(f32[5,3,36,148]{3,2,1,0:T(8,128)S(1)} %pad_maximum_fusion, f32[]{:T(128)} %bitcast.51, f32[]{:T(128)} %bitcast.50, f32[]{:T(128)} %bitcast.49, f32[]{:T(128)} %bitcast.48, f32[]{:T(128)} %bitcast.47, f32[]{:T(128)} %bitcast.46, f32[]{:T(128)} %bitcast.45, f32[]{:T(128)} %bitcast.44, f32[]{:T(128)} %bitcast.43, ...), kind=kLoop, calls=%fused_computation.138 | loop fusion | flops 1564920 | bytes 3577004 | tf_op jit(solution)/shard_map/add | solution.py:132
  153.4 7.4 %fusion.84 = f32[5,3,26,138]{3,2,1,0:T(8,128)S(1)} fusion(f32[5,3,36,138]{3,2,1,0:T(8,128)S(1)} %fusion.74, f32[]{:T(128)} %bitcast.51, f32[]{:T(128)} %bitcast.50, f32[]{:T(128)} %bitcast.49, f32[]{:T(128)} %bitcast.48, f32[]{:T(128)} %bitcast.47, f32[]{:T(128)} %bitcast.46, f32[]{:T(128)} %bitcast.45, f32[]{:T(128)} %bitcast.44, f32[]{:T(128)} %bitcast.43, ...), kind=kLoop, calls=%fused_computation.160 | loop fusion | flops 1130220 | bytes 2583404 | tf_op jit(solution)/shard_map/add | solution.py:135
  161.1 7.2 %fusion.98 = f32[3,3,26,128]{3,2,1,0:T(8,128)S(1)} fusion(f32[3,3,26,138]{3,2,1,0:T(8,128)S(1)} %maximum_multiply_fusion, f32[]{:T(128)} %bitcast.51, f32[]{:T(128)} %bitcast.50, f32[]{:T(128)} %bitcast.49, f32[]{:T(128)} %bitcast.48, f32[]{:T(128)} %bitcast.47, f32[]{:T(128)} %bitcast.46, f32[]{:T(128)} %bitcast.45, f32[]{:T(128)} %bitcast.44, ...), kind=kLoop, calls=%fused_computation.193 | loop fusion | flops 628992 | bytes 1437740 | tf_op jit(solution)/shard_map/add | solution.py:132
  168.3 6.9 %fusion.117 = f32[3,3,16,128]{3,2,1,0:T(8,128)S(1)} fusion(f32[3,3,26,128]{3,2,1,0:T(8,128)S(1)} %fusion.98, f32[]{:T(128)} %bitcast.51, f32[]{:T(128)} %bitcast.50, f32[]{:T(128)} %bitcast.49, f32[]{:T(128)} %bitcast.48, f32[]{:T(128)} %bitcast.47, f32[]{:T(128)} %bitcast.46, f32[]{:T(128)} %bitcast.45, f32[]{:T(128)} %bitcast.44, f32[]{:T(128)} %bitcast.43, ...), kind=kLoop, calls=%fused_computation.238 | loop fusion | flops 387072 | bytes 884780 | tf_op jit(solution)/shard_map/add | solution.py:135
  176.1 43.1 %while.25 = (s32[]{:T(128)}, f32[48,9,128]{2,1,0:T(8,128)S(1)}, s32[]{:T(128)}, f32[48,4,256]{2,0,1:T(8,128)S(1)}, f32[48,9,128]{2,1,0:T(8,128)S(1)}, /*index=5*...) while((s32[]{:T(128)}, f32[48,9,128]{2,1,0:T(8,128)S(1)}, ...), condition=%wide.region_14.15_spmd, body=%wide.region_7.0_spmd.sunk | while | flops 106244616 | bytes 1247007 | solution.py:172
  219.5 1.1 copy.69
  220.6 34.3 %scatter_custom_fusion = f32[9,1024]{0,1:T(8,128)} fusion(s32[6144]{0:T(1024)} %bitcast.222, f32[6144,9]{1,0:T(8,128)S(1)} %copy.69, f32[]{:T(128)} %constant.207.clone.1), kind=kCustom, calls=%fused_computation.184 | custom fusion | flops 55296 | bytes 37376 | tf_op jit(solution)/shard_map/scatter-add | solution.py:226
  254.8 1.3 copy.70
  256.2 100.8 %all_to_all.24 = f32[16,1,576]{2,1,0:T(1,128)S(1)} all-to-all(f32[16,1,576]{2,1,0:T(1,128)S(1)} %reshape.455), channel_id=1, replica_groups=mesh['gauss'=16,'tile'=2] {'gauss'}, dimensions={0} | all-to-all | bytes 73728 | tf_op jit(solution)/shard_map/all_to_all | solution.py:227
  358.2 3.2 scatter_custom_fusion.1
  (366 shorter events, 55.1 us)
Async XLA Ops:
  3.3 1.0 copy-start.2
  9.0 14.1 %all-to-all-start = ((f32[16,1,576]{2,1,0:T(1,128)}), f32[16,1,576]{2,1,0:T(1,128)S(1)}, u32[]{:S(2)}, u32[]{:S(2)}) async-start(f32[16,1,576]{2,1,0:T(1,128)} %reshape.453), calls=%async_computation | async-start | bytes 81920 | tf_op jit(solution)/shard_map/all_to_all | solution.py:181
  17.2 6.4 %copy-start.6 = (s32[6144,1]{0,1:T(1,128)}, s32[6144,1]{0,1:T(1,128)S(1)}, u32[]{:S(2)}) copy-start(s32[6144,1]{0,1:T(1,128)S(1)} %compare_select_fusion) | copy-start | bytes 73732
  50.3 24.8 %copy-start.7 = (s32[1,48]{1,0:T(1,128)S(1)}, s32[1,48]{1,0:T(1,128)}, u32[]{:S(2)}) copy-start(s32[1,48]{1,0:T(1,128)} %param.14) | copy-start | bytes 580
  50.3 25.6 %copy-start.1 = (f32[3,16,128]{2,1,0:T(8,128)S(1)}, f32[3,16,128]{2,1,0:T(8,128)}, u32[]{:S(2)}) copy-start(f32[3,16,128]{2,1,0:T(8,128)} %param.15) | copy-start | bytes 73732
  75.9 56.3 %collective-permute-start = (f32[2,3,10,128]{3,2,1,0:T(8,128)S(1)}, f32[2,3,10,128]{3,2,1,0:T(8,128)S(1)}, u32[]{:S(2)}, u32[]{:S(2)}) collective-permute-start(f32[2,3,10,128]{3,2,1,0:T(8,128)S(1)} %get-tuple-element.234), channel_id=1, source_target_pairs={{0,2},{2,4},{4,6},{6,8},{8,10},{10,12},{12,14},{14,16},{16,18},{18... | collective-permute-start | bytes 92168 | tf_op jit(solution)/shard_map/ppermute | solution.py:39
  130.2 3.4 collective-permute-start.1
  133.7 6.1 %collective-permute-start.2 = (f32[2,3,36,10]{3,2,1,0:T(8,128)S(1)}, f32[2,3,36,10]{3,2,1,0:T(8,128)S(1)}, u32[]{:S(2)}, u32[]{:S(2)}) collective-permute-start(f32[2,3,36,10]{3,2,1,0:T(8,128)S(1)} %get-tuple-element.216), channel_id=1, source_target_pairs={{0,1},{2,3},{4,5},{6,7},{8,9},{10,11},{12,13},{14,15},{16,17},{18,... | collective-permute-start | bytes 25928 | tf_op jit(solution)/shard_map/ppermute | solution.py:39
  136.7 7.9 %collective-permute-start.3 = (f32[2,3,36,10]{3,2,1,0:T(8,128)S(1)}, f32[2,3,36,10]{3,2,1,0:T(8,128)S(1)}, u32[]{:S(2)}, u32[]{:S(2)}) collective-permute-start(f32[2,3,36,10]{3,2,1,0:T(8,128)S(1)} %get-tuple-element.217), channel_id=1, source_target_pairs={{1,0},{3,2},{5,4},{7,6},{9,8},{11,10},{13,12},{15,14},{17,16},{19,... | collective-permute-start | bytes 25928 | tf_op jit(solution)/shard_map/ppermute | solution.py:41
  138.8 36.4 %copy-start.5 = (f32[3,16,128]{2,1,0:T(8,128)}, f32[3,16,128]{2,1,0:T(8,128)S(1)}, u32[]{:S(2)}) copy-start(f32[3,16,128]{2,1,0:T(8,128)S(1)} %reshape.407) | copy-start | bytes 73732
  220.5 141.3 %copy-start = (f32[48,1024]{1,0:T(8,128)S(1)}, f32[48,1024]{1,0:T(8,128)}, u32[]{:S(2)}) copy-start(f32[48,1024]{1,0:T(8,128)} %param.11) | copy-start | bytes 589828
  220.5 141.3 %copy-start.3 = (f32[16,1024]{1,0:T(8,128)S(1)}, f32[16,1024]{1,0:T(8,128)}, u32[]{:S(2)}) copy-start(f32[16,1024]{1,0:T(8,128)} %copy-done.2) | copy-start | bytes 196612
  220.5 142.0 %copy-start.4 = (f32[9,1024]{1,0:T(8,128)S(1)}, f32[9,1024]{1,0:T(8,128)}, u32[]{:S(2)}) copy-start(f32[9,1024]{1,0:T(8,128)} %param.10) | copy-start | bytes 110596
where the time goes:
time: 366 us; the launch traced here: 364 us
  blocking collectives  101 us (28%)
  other arithmetic  89.2 us (24%)
  starting transfers between devices  67.2 us (18%)
  local copies, waits for them, and re-layouts  37.4 us (10%)
  matrix products  32.3 us (9%)
  loops' own time  24.5 us (7%)
  waiting for transfers between devices  11 us (3%)
    all_to_all x1, blocking collectives, body(): lax.all_to_all(table_grad, 'gauss', split_axis=1, concat_axis=1, tiled=True)  101 us
    ppermute x2, starting transfers between devices, extended(): lax.ppermute(tail, axis, [(i, (i + 1) % count) for i in range(ends)])  57.3 us
    scatter-add x1, other arithmetic, body(): jnp.zeros_like(received).at[:, slot_rows.reshape(-1)].add(flat_grad)  34.3 us
    another operation x2, loops' own time, run_live(): return lax.fori_loop(0, live, advance, jnp.zeros(out_shape, jnp.float32))  24.5 us
    dot_general x45, matrix products, composite(): jnp.dot(earlier_mask, logged, precision=HIGHEST, preferred_element_type=j...  19.3 us
    gather x1, local copies, waits for them, and re-layouts, body(): received[:, slot_rows.reshape(-1)]  17.1 us
    add x2, other arithmetic, blur(): across = across + weights[offset] * padded[..., :, offset:offset + cols_out]  15.7 us
    add x2, other arithmetic, blur(): result = result + weights[offset] * across[..., offset:offset + rows_out, :]  14.3 us
  transfers between devices with their start and end apart: 5, of which 4 were waited for; matrix products, arithmetic and copies ran while one was open for 1% of the time, Pallas kernels for 0%

commit v1 on v0

--- a/solution.py
+++ b/solution.py
@@ -224,7 +224,9 @@
     block_grad = run_live(block_pullback, (per_block, results_grad), live, per_block.shape)
     flat_grad = jnp.moveaxis(block_grad, 0, 1).reshape(9, -1)
     table_grad = jnp.zeros_like(received).at[:, slot_rows.reshape(-1)].add(flat_grad)
-    back_records = lax.all_to_all(table_grad, "gauss", split_axis=1, concat_axis=1, tiled=True)
+    shards = jnp.split(table_grad, lax.axis_size("gauss"), axis=1)
+    got = lax.all_to_all(jnp.stack(shards), "gauss", 0, 0)
+    back_records = jnp.concatenate(got, axis=1)
     own_grad = jnp.zeros_like(own_records).at[:, send_list].set(back_records)
     unused_colour, shade_pull = jax.vjp(shade, splats[6:9], sh_coeffs)
     dir_grad, grad_sh = shade_pull(own_grad[6:9])

time: 366 us -> 378 us (1.033)
  local copies, waits for them, and re-layouts: 37.4 us -> 48.5 us
    unnamed x22 -> x37, local copies, waits for them, and re-layouts: 1.2 us -> 12.6 us
where the time goes in v1:
time: 378 us; the launch traced here: 375 us
  blocking collectives  101 us (27%)
  other arithmetic  89.2 us (24%)
  starting transfers between devices  67.2 us (18%)
  local copies, waits for them, and re-layouts  48.5 us (13%)
  matrix products  32.3 us (9%)
  loops' own time  24.5 us (6%)
  waiting for transfers between devices  11 us (3%)
    all_to_all x1, blocking collectives, body(): got = lax.all_to_all(jnp.stack(shards), 'gauss', 0, 0)  101 us
    ppermute x2, starting transfers between devices, extended(): lax.ppermute(tail, axis, [(i, (i + 1) % count) for i in range(ends)])  57.3 us
    scatter-add x1, other arithmetic, body(): jnp.zeros_like(received).at[:, slot_rows.reshape(-1)].add(flat_grad)  34.3 us
    another operation x2, loops' own time, run_live(): return lax.fori_loop(0, live, advance, jnp.zeros(out_shape, jnp.float32))  24.5 us
    dot_general x45, matrix products, composite(): jnp.dot(earlier_mask, logged, precision=HIGHEST, preferred_element_type=j...  19.3 us
    gather x1, local copies, waits for them, and re-layouts, body(): received[:, slot_rows.reshape(-1)]  17.1 us
    add x2, other arithmetic, blur(): across = across + weights[offset] * padded[..., :, offset:offset + cols_out]  15.7 us
    add x2, other arithmetic, blur(): result = result + weights[offset] * across[..., offset:offset + rows_out, :]  14.3 us
  transfers between devices with their start and end apart: 5, of which 4 were waited for; matrix products, arithmetic and copies ran while one was open for 1% of the time, Pallas kernels for 0%

profile of v1, /device:TPU:0, one launch (start us, length us, event | category | flops | bytes accessed | tf_op | source)
XLA Modules:
  0.0 374.8 jit_solution(17849110398606948401)
XLA Ops:
  0.6 0.9 multiply_multiply_fusion.2
  1.5 0.8 slice.409
  2.3 0.9 multiply_multiply_fusion.3
  3.3 1.0 multiply_reduce_fusion.2
  5.3 2.8 gather_fusion
  9.0 7.4 %all-to-all-start = ((f32[16,1,576]{2,1,0:T(1,128)}), f32[16,1,576]{2,1,0:T(1,128)S(1)}, u32[]{:S(2)}, u32[]{:S(2)}) async-start(f32[16,1,576]{2,1,0:T(1,128)} %reshape.459), calls=%async_computation | async-start | bytes 81920 | tf_op jit(solution)/shard_map/all_to_all | solution.py:181
  16.4 0.8 compare_select_fusion
  17.3 1.4 multiply_convert_fusion
  19.3 3.8 %all-to-all-done = f32[16,1,576]{2,1,0:T(1,128)S(1)} async-done(((f32[16,1,576]{2,1,0:T(1,128)}), f32[16,1,576]{2,1,0:T(1,128)S(1)}, u32[]{:S(2)}, u32[]{:S(2)}) %all-to-all-start) | async-done | bytes 36896 | tf_op jit(solution)/shard_map/all_to_all | solution.py:181
  24.5 1.0 copy.109
  25.5 17.1 %gather_fusion.1 = f32[6144,9]{1,0:T(8,128)S(1)} fusion(f32[9,1024]{0,1:T(8,128)} %bitcast.256, s32[6144]{0:T(1024)S(1)} %broadcast_clamp_fusion), kind=kCustom, calls=%fused_computation.1 | custom fusion | bytes 466944 | tf_op jit(solution)/shard_map/gather | solution.py:187
  42.6 2.5 slice.497
  45.2 2.5 slice_reduce_fusion
  47.7 2.4 copy.112
  50.3 24.7 %while.24 = (s32[]{:T(128)}, f32[48,4,256]{2,1,0:T(4,128)S(1)}, s32[]{:T(128)}, f32[48,9,128]{2,1,0:T(8,128)S(1)}, s32[]{:T(128)}, /*index=5*/s32[]{:T(128)}, s3...) while((s32[]{:T(128)}, f32[48,4,256]{2,1,0:T(4,128)S(1)}, s32[]{:T(128)}, f32[48,9,128]{2,1,0:T(8,128)S(1)}, ...), condition=%wide.region_4.5_spmd, body=%wide.region_2.4_spmd.sunk | while | flops 52843144 | bytes 296203 | solution.py:172
  75.9 54.4 %collective-permute-start = (f32[2,3,10,128]{3,2,1,0:T(8,128)S(1)}, f32[2,3,10,128]{3,2,1,0:T(8,128)S(1)}, u32[]{:S(2)}, u32[]{:S(2)}) collective-permute-start(f32[2,3,10,128]{3,2,1,0:T(8,128)S(1)} %get-tuple-element.239), channel_id=1, source_target_pairs={{0,2},{2,4},{4,6},{6,8},{8,10},{10,12},{12,14},{14,16},{16,18},{18... | collective-permute-start | bytes 92168 | tf_op jit(solution)/shard_map/ppermute | solution.py:39
  130.2 1.3 collective-permute-start.1
  132.1 1.5 collective-permute-done.1
  133.7 2.9 collective-permute-start.2
  136.7 1.3 collective-permute-start.3
  138.8 1.1 collective-permute-done.2
  139.9 4.7 %collective-permute-done.3 = f32[2,3,36,10]{3,2,1,0:T(8,128)S(1)} collective-permute-done((f32[2,3,36,10]{3,2,1,0:T(8,128)S(1)}, f32[2,3,36,10]{3,2,1,0:T(8,128)S(1)}, u32[]{:S(2)}, u32[]{:S(2)}) %collective-permute-start.3) | collective-permute-done | bytes 8672 | tf_op jit(solution)/shard_map/ppermute | solution.py:41
  145.0 8.4 %fusion.74 = f32[5,3,36,138]{3,2,1,0:T(8,128)S(1)} fusion(f32[5,3,36,148]{3,2,1,0:T(8,128)S(1)} %pad_maximum_fusion, f32[]{:T(128)} %bitcast.51, f32[]{:T(128)} %bitcast.50, f32[]{:T(128)} %bitcast.49, f32[]{:T(128)} %bitcast.48, f32[]{:T(128)} %bitcast.47, f32[]{:T(128)} %bitcast.46, f32[]{:T(128)} %bitcast.45, f32[]{:T(128)} %bitcast.44, f32[]{:T(128)} %bitcast.43, ...), kind=kLoop, calls=%fused_computation.138 | loop fusion | flops 1564920 | bytes 3577004 | tf_op jit(solution)/shard_map/add | solution.py:132
  153.4 7.4 %fusion.84 = f32[5,3,26,138]{3,2,1,0:T(8,128)S(1)} fusion(f32[5,3,36,138]{3,2,1,0:T(8,128)S(1)} %fusion.74, f32[]{:T(128)} %bitcast.51, f32[]{:T(128)} %bitcast.50, f32[]{:T(128)} %bitcast.49, f32[]{:T(128)} %bitcast.48, f32[]{:T(128)} %bitcast.47, f32[]{:T(128)} %bitcast.46, f32[]{:T(128)} %bitcast.45, f32[]{:T(128)} %bitcast.44, f32[]{:T(128)} %bitcast.43, ...), kind=kLoop, calls=%fused_computation.160 | loop fusion | flops 1130220 | bytes 2583404 | tf_op jit(solution)/shard_map/add | solution.py:135
  161.1 7.2 %fusion.98 = f32[3,3,26,128]{3,2,1,0:T(8,128)S(1)} fusion(f32[3,3,26,138]{3,2,1,0:T(8,128)S(1)} %maximum_multiply_fusion, f32[]{:T(128)} %bitcast.51, f32[]{:T(128)} %bitcast.50, f32[]{:T(128)} %bitcast.49, f32[]{:T(128)} %bitcast.48, f32[]{:T(128)} %bitcast.47, f32[]{:T(128)} %bitcast.46, f32[]{:T(128)} %bitcast.45, f32[]{:T(128)} %bitcast.44, ...), kind=kLoop, calls=%fused_computation.193 | loop fusion | flops 628992 | bytes 1437740 | tf_op jit(solution)/shard_map/add | solution.py:132
  168.3 6.9 %fusion.117 = f32[3,3,16,128]{3,2,1,0:T(8,128)S(1)} fusion(f32[3,3,26,128]{3,2,1,0:T(8,128)S(1)} %fusion.98, f32[]{:T(128)} %bitcast.51, f32[]{:T(128)} %bitcast.50, f32[]{:T(128)} %bitcast.49, f32[]{:T(128)} %bitcast.48, f32[]{:T(128)} %bitcast.47, f32[]{:T(128)} %bitcast.46, f32[]{:T(128)} %bitcast.45, f32[]{:T(128)} %bitcast.44, f32[]{:T(128)} %bitcast.43, ...), kind=kLoop, calls=%fused_computation.238 | loop fusion | flops 387072 | bytes 884780 | tf_op jit(solution)/shard_map/add | solution.py:135
  176.1 43.1 %while.25 = (s32[]{:T(128)}, f32[48,9,128]{2,1,0:T(8,128)S(1)}, s32[]{:T(128)}, f32[48,4,256]{2,0,1:T(8,128)S(1)}, f32[48,9,128]{2,1,0:T(8,128)S(1)}, /*index=5*...) while((s32[]{:T(128)}, f32[48,9,128]{2,1,0:T(8,128)S(1)}, ...), condition=%wide.region_14.15_spmd, body=%wide.region_7.0_spmd.sunk | while | flops 106244616 | bytes 1247007 | solution.py:172
  219.5 1.1 copy.119
  220.6 34.3 %scatter_custom_fusion = f32[9,1024]{0,1:T(8,128)} fusion(s32[6144]{0:T(1024)} %bitcast.282, f32[6144,9]{1,0:T(8,128)S(1)} %copy.119, f32[]{:T(128)} %constant.207.clone.1), kind=kCustom, calls=%fused_computation.184 | custom fusion | flops 55296 | bytes 37376 | tf_op jit(solution)/shard_map/scatter-add | solution.py:226
  257.1 0.8 fusion.143
  267.3 100.8 %all_to_all.17 = f32[16,1,576]{2,1,0:T(1,128)S(1)} all-to-all(f32[16,1,576]{2,1,0:T(1,128)S(1)} %reshape.461), channel_id=1, replica_groups=mesh['gauss'=16,'tile'=2] {'gauss'}, dimensions={0} | all-to-all | bytes 73728 | tf_op jit(solution)/shard_map/all_to_all | solution.py:228
  369.3 3.2 scatter_custom_fusion.1
  (382 shorter events, 66.7 us)
Async XLA Ops:
  3.3 1.0 copy-start.2
  9.0 14.1 %all-to-all-start = ((f32[16,1,576]{2,1,0:T(1,128)}), f32[16,1,576]{2,1,0:T(1,128)S(1)}, u32[]{:S(2)}, u32[]{:S(2)}) async-start(f32[16,1,576]{2,1,0:T(1,128)} %reshape.459), calls=%async_computation | async-start | bytes 81920 | tf_op jit(solution)/shard_map/all_to_all | solution.py:181
  17.2 6.4 %copy-start.6 = (s32[6144,1]{0,1:T(1,128)}, s32[6144,1]{0,1:T(1,128)S(1)}, u32[]{:S(2)}) copy-start(s32[6144,1]{0,1:T(1,128)S(1)} %compare_select_fusion) | copy-start | bytes 73732
  50.3 24.8 %copy-start.7 = (s32[1,48]{1,0:T(1,128)S(1)}, s32[1,48]{1,0:T(1,128)}, u32[]{:S(2)}) copy-start(s32[1,48]{1,0:T(1,128)} %param.14) | copy-start | bytes 580
  50.3 25.6 %copy-start.1 = (f32[3,16,128]{2,1,0:T(8,128)S(1)}, f32[3,16,128]{2,1,0:T(8,128)}, u32[]{:S(2)}) copy-start(f32[3,16,128]{2,1,0:T(8,128)} %param.15) | copy-start | bytes 73732
  75.9 56.3 %collective-permute-start = (f32[2,3,10,128]{3,2,1,0:T(8,128)S(1)}, f32[2,3,10,128]{3,2,1,0:T(8,128)S(1)}, u32[]{:S(2)}, u32[]{:S(2)}) collective-permute-start(f32[2,3,10,128]{3,2,1,0:T(8,128)S(1)} %get-tuple-element.239), channel_id=1, source_target_pairs={{0,2},{2,4},{4,6},{6,8},{8,10},{10,12},{12,14},{14,16},{16,18},{18... | collective-permute-start | bytes 92168 | tf_op jit(solution)/shard_map/ppermute | solution.py:39
  130.2 3.4 collective-permute-start.1
  133.7 6.1 %collective-permute-start.2 = (f32[2,3,36,10]{3,2,1,0:T(8,128)S(1)}, f32[2,3,36,10]{3,2,1,0:T(8,128)S(1)}, u32[]{:S(2)}, u32[]{:S(2)}) collective-permute-start(f32[2,3,36,10]{3,2,1,0:T(8,128)S(1)} %get-tuple-element.221), channel_id=1, source_target_pairs={{0,1},{2,3},{4,5},{6,7},{8,9},{10,11},{12,13},{14,15},{16,17},{18,... | collective-permute-start | bytes 25928 | tf_op jit(solution)/shard_map/ppermute | solution.py:39
  136.7 7.9 %collective-permute-start.3 = (f32[2,3,36,10]{3,2,1,0:T(8,128)S(1)}, f32[2,3,36,10]{3,2,1,0:T(8,128)S(1)}, u32[]{:S(2)}, u32[]{:S(2)}) collective-permute-start(f32[2,3,36,10]{3,2,1,0:T(8,128)S(1)} %get-tuple-element.222), channel_id=1, source_target_pairs={{1,0},{3,2},{5,4},{7,6},{9,8},{11,10},{13,12},{15,14},{17,16},{19,... | collective-permute-start | bytes 25928 | tf_op jit(solution)/shard_map/ppermute | solution.py:41
  138.8 36.4 %copy-start.5 = (f32[3,16,128]{2,1,0:T(8,128)}, f32[3,16,128]{2,1,0:T(8,128)S(1)}, u32[]{:S(2)}) copy-start(f32[3,16,128]{2,1,0:T(8,128)S(1)} %reshape.411) | copy-start | bytes 73732
  220.5 152.4 %copy-start = (f32[48,1024]{1,0:T(8,128)S(1)}, f32[48,1024]{1,0:T(8,128)}, u32[]{:S(2)}) copy-start(f32[48,1024]{1,0:T(8,128)} %param.11) | copy-start | bytes 589828
  220.5 152.4 %copy-start.3 = (f32[16,1024]{1,0:T(8,128)S(1)}, f32[16,1024]{1,0:T(8,128)}, u32[]{:S(2)}) copy-start(f32[16,1024]{1,0:T(8,128)} %copy-done.2) | copy-start | bytes 196612
  220.5 153.1 %copy-start.4 = (f32[9,1024]{1,0:T(8,128)S(1)}, f32[9,1024]{1,0:T(8,128)}, u32[]{:S(2)}) copy-start(f32[9,1024]{1,0:T(8,128)} %param.10) | copy-start | bytes 110596
